TPU v7x, 128 devices: a whole 4x4x4 slice. The times are simulated.
128 devices in a mesh: ctx: 16 (over y_lo, x, core), exp: 8 (over y_hi, z).
Axes of the slice: x: 4, y: 4 (y_hi: 2, y_lo: 2; y = y_hi * 2 + y_lo), z: 4, core: 2. Of those that a mesh axis runs over, the one named last changes fastest.
Arguments:
- queries: bfloat16 [2048, 3072], P('ctx', 'exp'), may hold values from -8 to 8
- keys: bfloat16 [2048, 1024], P('ctx', 'exp'), may hold values from -8 to 8
- values: bfloat16 [2048, 1024], P('ctx', 'exp'), may hold values from -6 to 6
- norm_gain: float32 [3072], replicated, may hold values from 0.1 to 1.9
- routes: int32 [2048, 2], P(('ctx', 'exp')), may hold values from 0 to 7, all different within a row; in each aligned block of 16 rows (0 to 15, 16 to 31, ...) at most 6 rows name the same one
- route_scores: float32 [2048, 2], P(('ctx', 'exp')), may hold values from -8 to 8
- cotangent: bfloat16 [2048, 3072], P(('ctx', 'exp')), may hold values from -6 to 6
- w_gate: bfloat16 [8, 3072, 8192], P('exp', None, 'ctx'), may hold values from -0.109375 to 0.109375
- w_up: bfloat16 [8, 3072, 8192], P('exp', None, 'ctx'), may hold values from -0.109375 to 0.109375
- w_down: bfloat16 [8, 8192, 3072], P('exp', 'ctx'), may hold values from -0.0625 to 0.0625
Outputs:
- mixed: bfloat16 [2048, 3072], P(('ctx', 'exp'))
- grad_input: bfloat16 [2048, 3072], P(('ctx', 'exp'))
- grad_gate: bfloat16 [8, 3072, 8192], P('exp', None, 'ctx')
- grad_up: bfloat16 [8, 3072, 8192], P('exp', None, 'ctx')
- grad_down: bfloat16 [8, 8192, 3072], P('exp', 'ctx')
Inputs may be any that keep to these rules, and one draw needn't show every extreme that they name: `routes`: each row names two different experts. Within each aligned block of 16 rows (the rows of one device) no expert is named by more than 6 rows, a bound that some block reaches.
All inputs are finite; a program needn't handle non-finite values.
Results may differ from a plain program's by a relative error of at most 0.018.
Values may be sent and summed in bfloat16 or wider, within the bound.
A program may use at most 128 MiB of HBM per device.

v0:
```python
import jax
import jax.numpy as jnp
from jax import lax
from jax.sharding import PartitionSpec as P

norm_eps = 1e-05
masked_value = -1e30


def heads_first(query_local, group, head):
    count = query_local.shape[0]
    return query_local.reshape(count, group, head).transpose(1, 0, 2).reshape(group * count, head)


def local(queries, keys, values, norm_gain, routes, route_scores, cotangent, w_gate, w_up, w_down):
    n_exp = lax.axis_size("exp")
    head = keys.shape[1]
    group = queries.shape[1] // head
    tok_ctx = queries.shape[0]
    ctx_index = lax.axis_index("ctx")
    query_flat = heads_first(queries, group, head)
    query_pos = ctx_index * tok_ctx + jnp.tile(jnp.arange(tok_ctx, dtype=jnp.int32), group)
    key_values = lax.all_gather(jnp.concatenate([keys, values], axis=1), "ctx", axis=0, tiled=True)
    scores = lax.dot_general(
        query_flat,
        key_values[:, :head],
        (((1,), (1,)), ((), ())),
        preferred_element_type=jnp.float32,
    ) * head ** (-0.5)
    allowed = jnp.arange(key_values.shape[0], dtype=jnp.int32)[None, :] <= query_pos[:, None]
    scores = jnp.where(allowed, scores, masked_value)
    weights = jnp.exp(scores - jnp.max(scores, axis=1, keepdims=True))
    totals = jnp.sum(weights, axis=1, keepdims=True)
    attended = (
        jnp.dot(
            weights.astype(jnp.bfloat16), key_values[:, head:], preferred_element_type=jnp.float32
        )
        / totals
    )
    attended = (
        attended.reshape(group, tok_ctx, head)
        .transpose(1, 0, 2)
        .reshape(tok_ctx, group * head)
        .astype(jnp.bfloat16)
    )
    features = lax.all_to_all(attended, "exp", split_axis=0, concat_axis=1, tiled=True)
    feats = features.astype(jnp.float32)
    inv_rms = lax.rsqrt(jnp.mean(feats * feats, axis=1) + norm_eps)
    normed = (feats * inv_rms[:, None] * norm_gain[None, :]).astype(jnp.bfloat16)
    tok_dev = normed.shape[0]
    width = normed.shape[1]
    capacity = 3 * tok_dev // n_exp
    slots = n_exp * capacity
    flat_routes = routes.reshape(-1)
    onehot = (flat_routes[:, None] == jnp.arange(n_exp, dtype=jnp.int32)[None, :]).astype(jnp.int32)
    ranks = jnp.sum((jnp.cumsum(onehot, axis=0) - onehot) * onehot, axis=1)
    target = flat_routes * capacity + ranks
    placed = (jnp.arange(slots, dtype=jnp.int32)[:, None] == target[None, :]).astype(jnp.float32)
    place_tokens = placed.reshape(slots, tok_dev, 2).sum(axis=2)
    probs = jax.nn.softmax(route_scores, axis=1)
    mixing = (placed * probs.reshape(-1)[None, :]).reshape(slots, tok_dev, 2).sum(axis=2)
    send = jnp.dot(
        place_tokens.astype(jnp.bfloat16), normed, preferred_element_type=jnp.float32
    ).astype(jnp.bfloat16)
    arrived = lax.all_to_all(
        send.reshape(n_exp, capacity, width), "exp", split_axis=0, concat_axis=0, tiled=True
    ).reshape(slots, width)
    expert_in = lax.all_gather(arrived, "ctx", axis=0, tiled=True)
    gate_w = w_gate[0]
    up_w = w_up[0]
    down_w = w_down[0]
    gate_pre = jnp.dot(expert_in, gate_w, preferred_element_type=jnp.float32)
    up_pre = jnp.dot(expert_in, up_w, preferred_element_type=jnp.float32)
    hidden = (jax.nn.silu(gate_pre) * up_pre).astype(jnp.bfloat16)
    expert_out = lax.psum_scatter(
        jnp.dot(hidden, down_w, preferred_element_type=jnp.float32).astype(jnp.bfloat16),
        "ctx",
        scatter_dimension=0,
        tiled=True,
    )
    returned = lax.all_to_all(
        expert_out.reshape(n_exp, capacity, width), "exp", split_axis=0, concat_axis=0, tiled=True
    ).reshape(slots, width)
    mixed = lax.dot_general(
        mixing,
        returned.astype(jnp.float32),
        (((0,), (0,)), ((), ())),
        precision=lax.Precision.HIGHEST,
    ).astype(jnp.bfloat16)
    grad_slots = jnp.dot(
        mixing, cotangent.astype(jnp.float32), precision=lax.Precision.HIGHEST
    ).astype(jnp.bfloat16)
    grad_arrived = lax.all_to_all(
        grad_slots.reshape(n_exp, capacity, width), "exp", split_axis=0, concat_axis=0, tiled=True
    ).reshape(slots, width)
    grad_out = lax.all_gather(grad_arrived, "ctx", axis=0, tiled=True)
    rows_in = expert_in
    grad_hidden = lax.dot_general(
        grad_out, down_w, (((1,), (1,)), ((), ())), preferred_element_type=jnp.float32
    )
    grad_down = lax.dot_general(
        hidden, grad_out, (((0,), (0,)), ((), ())), preferred_element_type=jnp.float32
    ).astype(jnp.bfloat16)
    sig = jax.nn.sigmoid(gate_pre)
    grad_up_pre = (grad_hidden * (gate_pre * sig)).astype(jnp.bfloat16)
    grad_gate_pre = (grad_hidden * up_pre * sig * (1.0 + gate_pre * (1.0 - sig))).astype(
        jnp.bfloat16
    )
    grad_gate = lax.dot_general(
        rows_in, grad_gate_pre, (((0,), (0,)), ((), ())), preferred_element_type=jnp.float32
    ).astype(jnp.bfloat16)
    grad_upw = lax.dot_general(
        rows_in, grad_up_pre, (((0,), (0,)), ((), ())), preferred_element_type=jnp.float32
    ).astype(jnp.bfloat16)
    term = lax.dot_general(
        grad_gate_pre, gate_w, (((1,), (1,)), ((), ())), preferred_element_type=jnp.float32
    )
    grad_summed = lax.psum_scatter(
        (
            term
            + lax.dot_general(
                grad_up_pre, up_w, (((1,), (1,)), ((), ())), preferred_element_type=jnp.float32
            )
        ).astype(jnp.bfloat16),
        "ctx",
        scatter_dimension=0,
        tiled=True,
    )
    grad_back = lax.all_to_all(
        grad_summed.reshape(n_exp, capacity, width), "exp", split_axis=0, concat_axis=0, tiled=True
    ).reshape(slots, width)
    grad_normed = lax.dot_general(
        place_tokens,
        grad_back.astype(jnp.float32),
        (((0,), (0,)), ((), ())),
        precision=lax.Precision.HIGHEST,
    )
    weighted = grad_normed * norm_gain[None, :]
    inner = jnp.mean(weighted * feats, axis=1)
    grad_input = (inv_rms[:, None] * weighted - feats * (inv_rms**3 * inner)[:, None]).astype(
        jnp.bfloat16
    )
    return (mixed, grad_input, grad_gate[None], grad_upw[None], grad_down[None])


def solution(mesh):
    placed = (
        P("ctx", "exp"),
        P("ctx", "exp"),
        P("ctx", "exp"),
        P(),
        P(("ctx", "exp"), None),
        P(("ctx", "exp"), None),
        P(("ctx", "exp"), None),
        P("exp", None, "ctx"),
        P("exp", None, "ctx"),
        P("exp", "ctx", None),
    )
    return jax.shard_map(
        local,
        mesh=mesh,
        in_specs=placed,
        out_specs=(
            P(("ctx", "exp"), None),
            P(("ctx", "exp"), None),
            P("exp", None, "ctx"),
            P("exp", None, "ctx"),
            P("exp", "ctx", None),
        ),
        check_vma=False,
    )
```

profile of v0, /device:TPU:16, one launch (start us, length us, event | category | flops | bytes accessed | tf_op | source)
XLA Modules:
  0.0 338.5 jit_solution(3207125207926384056)
XLA Ops:
  7.2 1.6 pad_maximum_fusion
  8.8 0.8 copy.35
  9.8 0.2 select_reduce_fusion.1
  10.2 1.0 copy.37
  11.3 0.7 reduce_max.18
  12.0 0.7 fusion.33
  12.7 0.7 fusion.32
  13.4 0.7 multiply_add_fusion
  14.1 30.5 %all-gather.4.cloned.1.call-done = bf16[2048,256]{1,0:T(8,128)(2,1)} async-done(((bf16[128,256]{1,0:T(8,128)(2,1)}), bf16[2048,256]{1,0:T(8,128)(2,1)}) %all-gather.4.cloned.1.call-update) | async-done | bytes 1048592 | tf_op jit(solution)/shard_map/all_gather | solution.py:23
  44.6 1.8 fusion.35
  46.4 0.5 fusion.13
  47.0 0.6 fusion.22
  47.7 0.7 convert_element_type.88
  48.5 7.4 %all-to-all-start = ((bf16[8,16,384]{2,1,0:T(8,128)(2,1)}), bf16[8,16,384]{2,1,0:T(8,128)(2,1)S(1)}, u32[]{:S(2)}, u32[]{:S(2)}) async-start(bf16[8,16,384]{2,1,0:T(8,128)(2,1)} %convert_element_type.88), calls=%async_computation | async-start | bytes 196608 | tf_op jit(solution)/shard_map/all_to_all | solution.py:46
  55.9 5.0 %all-to-all-done = bf16[8,16,384]{2,1,0:T(8,128)(2,1)S(1)} async-done(((bf16[8,16,384]{2,1,0:T(8,128)(2,1)}), bf16[8,16,384]{2,1,0:T(8,128)(2,1)S(1)}, u32[]{:S(2)}, u32[]{:S(2)}) %all-to-all-start) | async-done | bytes 98336 | tf_op jit(solution)/shard_map/all_to_all | solution.py:46
  60.9 0.1 fusion.27
  61.1 1.0 convolution_convert_fusion.5
  62.1 1.8 reshape.111
  63.9 13.6 %all_to_all.30 = bf16[8,6,3072]{2,1,0:T(8,128)(2,1)} all-to-all(bf16[8,6,3072]{2,1,0:T(8,128)(2,1)} %reshape.111), channel_id=1, replica_groups=mesh['ctx'=16,'exp'=8] {'exp'}, dimensions={0} | all-to-all | bytes 589824 | tf_op jit(solution)/shard_map/all_to_all | solution.py:65
  77.5 1.8 reshape.112
  79.4 1.2 convolution_convert_fusion.4
  80.6 1.8 reshape.115
  82.4 18.0 %all_to_all.31 = bf16[8,6,3072]{2,1,0:T(8,128)(2,1)} all-to-all(bf16[8,6,3072]{2,1,0:T(8,128)(2,1)} %reshape.115), channel_id=1, replica_groups=mesh['ctx'=16,'exp'=8] {'exp'}, dimensions={0} | all-to-all | bytes 589824 | tf_op jit(solution)/shard_map/all_to_all | solution.py:93
  100.4 1.8 reshape.116
  102.2 16.1 %all-gather.6.cloned.1.call-done = bf16[768,3072]{1,0:T(8,128)(2,1)} async-done(((bf16[48,3072]{1,0:T(8,128)(2,1)}), bf16[768,3072]{1,0:T(8,128)(2,1)}) %all-gather.6.cloned.1.call-update) | async-done | bytes 4718608 | tf_op jit(solution)/shard_map/all_gather | solution.py:68
  118.4 7.2 %fusion.7 = f32[768,512]{1,0:T(8,128)} fusion(bf16[768,3072]{1,0:T(8,128)(2,1)} %all-gather.6.cloned.1.call-done, bf16[1,3072,512]{2,1,0:T(8,128)(2,1)} %param.18), kind=kOutput, calls=%fused_computation.16 | convolution fusion | flops 2415919104 | bytes 9437184 | tf_op jit(solution)/shard_map/dot_general | solution.py:73
  125.6 3.7 %fusion.11 = f32[768,512]{1,0:T(8,128)} fusion(bf16[768,3072]{1,0:T(8,128)(2,1)S(1)} %copy-done.6, bf16[1,3072,512]{2,1,0:T(8,128)(2,1)S(1)} %copy-done.7), kind=kOutput, calls=%fused_computation.20 | convolution fusion | flops 2415919104 | bytes 9437184 | tf_op jit(solution)/shard_map/dot_general | solution.py:72
  129.3 30.0 %all-gather.8.cloned.1.call-done = bf16[768,3072]{1,0:T(8,128)(2,1)} async-done(((bf16[48,3072]{1,0:T(8,128)(2,1)}), bf16[768,3072]{1,0:T(8,128)(2,1)}) %all-gather.8.cloned.1.call-update) | async-done | bytes 4718608 | tf_op jit(solution)/shard_map/all_gather | solution.py:96
  159.3 7.0 %multiply_convert_fusion = (bf16[768,512]{1,0:T(8,128)(2,1)}, bf16[768,512]{1,0:T(8,128)(2,1)}, bf16[768,512]{1,0:T(8,128)(2,1)S(1)}) fusion(f32[768,512]{1,0:T(8,128)} %fusion.11, f32[768,512]{1,0:T(8,128)} %fusion.7, bf16[768,3072]{1,0:T(8,128)(2,1)} %all-gather.8.cloned.1.call-done, bf16[1,512,3072]{2,1,0:T(8,128)(2,1)S(1)} %copy-done), kind=kOutput, calls=%fused_computation.28 | convolution fusion | flops 2421817344 | bytes 13369344 | tf_op jit(solution)/shard_map/dot_general | solution.py:98
  166.3 0.9 copy-done.8
  167.2 4.2 %convolution_convert_fusion = bf16[768,3072]{1,0:T(8,128)(2,1)} fusion(bf16[768,512]{1,0:T(8,128)(2,1)S(1)} %get-tuple-element.9, bf16[1,512,3072]{2,1,0:T(8,128)(2,1)S(1)} %copy-done), kind=kOutput, calls=%fused_computation.1 | convolution fusion | flops 2418278400 | bytes 8650752 | tf_op jit(solution)/shard_map/dot_general | solution.py:76
  171.5 0.2 reduce-scatter.5.cloned.1.call-start
  171.7 4.9 %fusion.9 = f32[768,3072]{1,0:T(8,128)S(1)} fusion(bf16[768,512]{1,0:T(8,128)(2,1)} %get-tuple-element.8, bf16[1,3072,512]{2,1,0:T(8,128)(2,1)} %param.17), kind=kOutput, calls=%fused_computation.18 | convolution fusion | flops 2415919104 | bytes 13369344 | tf_op jit(solution)/shard_map/dot_general | solution.py:115
  176.6 4.4 %add_convert_fusion = bf16[768,3072]{1,0:T(8,128)(2,1)} fusion(f32[768,3072]{1,0:T(8,128)S(1)} %fusion.9, bf16[768,512]{1,0:T(8,128)(2,1)S(1)} %copy-done.2, bf16[1,3072,512]{2,1,0:T(8,128)(2,1)S(1)} %copy-done.1), kind=kOutput, calls=%fused_computation | convolution fusion | flops 2420637696 | bytes 18087936 | tf_op jit(solution)/shard_map/dot_general | solution.py:121
  181.1 6.9 %fusion.2 = bf16[1,512,3072]{2,1,0:T(8,128)(2,1)} fusion(bf16[768,512]{1,0:T(8,128)(2,1)} %copy-done.8, bf16[768,3072]{1,0:T(8,128)(2,1)} %all-gather.8.cloned.1.call-done), kind=kOutput, calls=%fused_computation.7 | convolution fusion | flops 2417491968 | bytes 8650752 | tf_op jit(solution)/shard_map/dot_general | solution.py:101
  188.0 51.4 %reduce-scatter.3.cloned.1.call-done = bf16[48,3072]{1,0:T(8,128)(2,1)} async-done(((bf16[768,3072]{1,0:T(8,128)(2,1)}), bf16[48,3072]{1,0:T(8,128)(2,1)}) %reduce-scatter.3.cloned.1.call-update) | async-done | bytes 294928 | tf_op jit(solution)/shard_map/reduce_scatter | solution.py:75
  239.4 1.8 reshape.113
  241.2 7.5 %all-to-all-start.2 = ((bf16[8,6,3072]{2,1,0:T(8,128)(2,1)}), bf16[8,6,3072]{2,1,0:T(8,128)(2,1)}, u32[]{:S(2)}, u32[]{:S(2)}) async-start(bf16[8,6,3072]{2,1,0:T(8,128)(2,1)} %reshape.113), calls=%async_computation.3 | async-start | bytes 786432 | tf_op jit(solution)/shard_map/all_to_all | solution.py:81
  248.7 7.0 %fusion.1 = bf16[1,3072,512]{2,1,0:T(8,128)(2,1)} fusion(bf16[768,3072]{1,0:T(8,128)(2,1)} %all-gather.6.cloned.1.call-done, bf16[768,512]{1,0:T(8,128)(2,1)} %get-tuple-element.7), kind=kOutput, calls=%fused_computation.6 | convolution fusion | flops 2417491968 | bytes 8650752 | tf_op jit(solution)/shard_map/dot_general | solution.py:112
  255.7 52.4 %reduce-scatter.5.cloned.1.call-done = bf16[48,3072]{1,0:T(8,128)(2,1)} async-done(((bf16[768,3072]{1,0:T(8,128)(2,1)}), bf16[48,3072]{1,0:T(8,128)(2,1)}) %reduce-scatter.5.cloned.1.call-update) | async-done | bytes 294928 | tf_op jit(solution)/shard_map/reduce_scatter | solution.py:118
  308.2 1.8 reshape.117
  310.0 7.5 %all-to-all-start.4 = ((bf16[8,6,3072]{2,1,0:T(8,128)(2,1)}), bf16[8,6,3072]{2,1,0:T(8,128)(2,1)}, u32[]{:S(2)}, u32[]{:S(2)}) async-start(bf16[8,6,3072]{2,1,0:T(8,128)(2,1)} %reshape.117), calls=%async_computation.6 | async-start | bytes 786432 | tf_op jit(solution)/shard_map/all_to_all | solution.py:129
  317.5 6.9 %fusion = bf16[1,3072,512]{2,1,0:T(8,128)(2,1)} fusion(bf16[768,3072]{1,0:T(8,128)(2,1)} %all-gather.6.cloned.1.call-done, bf16[768,512]{1,0:T(8,128)(2,1)} %get-tuple-element.8), kind=kOutput, calls=%fused_computation.5 | convolution fusion | flops 2417491968 | bytes 8650752 | tf_op jit(solution)/shard_map/dot_general | solution.py:109
  324.4 1.8 reshape.114
  326.2 1.9 convolution_convert_fusion.6
  328.1 1.8 reshape.118
  329.9 1.3 multiply_reduce_fusion
  331.2 0.7 subtract_convert_fusion
  (41 shorter events, 1.0 us)
Async XLA Ops:
  7.2 152.1 %copy-start = (bf16[1,512,3072]{2,1,0:T(8,128)(2,1)S(1)}, bf16[1,512,3072]{2,1,0:T(8,128)(2,1)}, u32[]{:S(2)}) copy-start(bf16[1,512,3072]{2,1,0:T(8,128)(2,1)} %param.19) | copy-start | bytes 9437188
  7.2 37.5 %all-gather.4.cloned.1.call-start = ((), (), s32[]{:S(2)}) async-start(), calls=%async_computation.7 | async-start | bytes 1114112 | tf_op jit(solution)/shard_map/all_gather | solution.py:23
  44.6 2.3 copy-start.3
  47.0 14.1 %copy-start.5 = (f32[3072]{0:T(1024)S(1)}, f32[3072]{0:T(1024)}, u32[]{:S(2)}) copy-start(f32[3072]{0:T(1024)} %param.13) | copy-start | bytes 36868
  47.6 31.8 %copy-start.4 = (bf16[16,3072]{1,0:T(8,128)(2,1)S(1)}, bf16[16,3072]{1,0:T(8,128)(2,1)}, u32[]{:S(2)}) copy-start(bf16[16,3072]{1,0:T(8,128)(2,1)} %param.16) | copy-start | bytes 294916
  48.5 12.5 %all-to-all-start = ((bf16[8,16,384]{2,1,0:T(8,128)(2,1)}), bf16[8,16,384]{2,1,0:T(8,128)(2,1)S(1)}, u32[]{:S(2)}, u32[]{:S(2)}) async-start(bf16[8,16,384]{2,1,0:T(8,128)(2,1)} %convert_element_type.88), calls=%async_computation | async-start | bytes 196608 | tf_op jit(solution)/shard_map/all_to_all | solution.py:46
  55.9 62.5 %all-gather.6.cloned.1.call-start = ((), (), s32[]{:S(2)}) async-start(), calls=%async_computation.8 | async-start | bytes 5013504 | tf_op jit(solution)/shard_map/all_gather | solution.py:68
  79.4 80.0 %all-gather.8.cloned.1.call-start = ((), (), s32[]{:S(2)}) async-start(), calls=%async_computation.10 | async-start | bytes 5013504 | tf_op jit(solution)/shard_map/all_gather | solution.py:96
  102.2 137.2 %reduce-scatter.3.cloned.1.call-start = ((), (), s32[]{:S(2)}) async-start(), calls=%async_computation.9 | async-start | bytes 5013504 | tf_op jit(solution)/shard_map/reduce_scatter | solution.py:75
  118.4 7.2 %copy-start.6 = (bf16[768,3072]{1,0:T(8,128)(2,1)S(1)}, bf16[768,3072]{1,0:T(8,128)(2,1)}, u32[]{:S(2)}) copy-start(bf16[768,3072]{1,0:T(8,128)(2,1)} %all-gather.6.cloned.1.call-done) | copy-start | bytes 14155780
  118.4 7.2 %copy-start.7 = (bf16[1,3072,512]{2,1,0:T(8,128)(2,1)S(1)}, bf16[1,3072,512]{2,1,0:T(8,128)(2,1)}, u32[]{:S(2)}) copy-start(bf16[1,3072,512]{2,1,0:T(8,128)(2,1)} %param.17) | copy-start | bytes 9437188
  166.3 0.9 copy-start.8
  171.5 136.7 %reduce-scatter.5.cloned.1.call-start = ((), (), s32[]{:S(2)}) async-start(), calls=%async_computation.11 | async-start | bytes 5013504 | tf_op jit(solution)/shard_map/reduce_scatter | solution.py:118
  171.7 4.9 %copy-start.1 = (bf16[1,3072,512]{2,1,0:T(8,128)(2,1)S(1)}, bf16[1,3072,512]{2,1,0:T(8,128)(2,1)}, u32[]{:S(2)}) copy-start(bf16[1,3072,512]{2,1,0:T(8,128)(2,1)} %param.18) | copy-start | bytes 9437188
  171.7 4.9 %copy-start.2 = (bf16[768,512]{1,0:T(8,128)(2,1)S(1)}, bf16[768,512]{1,0:T(8,128)(2,1)}, u32[]{:S(2)}) copy-start(bf16[768,512]{1,0:T(8,128)(2,1)} %get-tuple-element.7) | copy-start | bytes 2359300
  241.2 68.8 %all-to-all-start.2 = ((bf16[8,6,3072]{2,1,0:T(8,128)(2,1)}), bf16[8,6,3072]{2,1,0:T(8,128)(2,1)}, u32[]{:S(2)}, u32[]{:S(2)}) async-start(bf16[8,6,3072]{2,1,0:T(8,128)(2,1)} %reshape.113), calls=%async_computation.3 | async-start | bytes 786432 | tf_op jit(solution)/shard_map/all_to_all | solution.py:81
  310.0 18.1 %all-to-all-start.4 = ((bf16[8,6,3072]{2,1,0:T(8,128)(2,1)}), bf16[8,6,3072]{2,1,0:T(8,128)(2,1)}, u32[]{:S(2)}, u32[]{:S(2)}) async-start(bf16[8,6,3072]{2,1,0:T(8,128)(2,1)} %reshape.117), calls=%async_computation.6 | async-start | bytes 786432 | tf_op jit(solution)/shard_map/all_to_all | solution.py:129
Sparse Core Ops, SparseCore 0:
  10.3 34.3 all-gather.3
  79.5 38.8 all-gather.5
  120.7 38.6 all-gather.7
  171.6 67.7 reduce-scatter.2
  241.6 66.4 reduce-scatter.4
where the time goes:
time: 340 us; the launch traced here: 338 us
  waiting for transfers between devices  186 us (55%)
  matrix products  60 us (18%)
  blocking collectives  31.6 us (9%)
  starting transfers between devices  22.8 us (7%)
  local copies, waits for them, and re-layouts  18.4 us (5%)
  between operations  13.9 us (4%)
  other arithmetic  6.2 us (2%)
    reduce_scatter x1, waiting for transfers between devices, local(): lax.psum_scatter((term + lax.dot_general(grad_up_pre, up_w, (((1,), (1,))...  52.4 us
    reduce_scatter x1, waiting for transfers between devices, local(): lax.psum_scatter(jnp.dot(hidden, down_w, preferred_element_type=jnp.float...  51.4 us
    all_gather x1, waiting for transfers between devices, local(): lax.all_gather(jnp.concatenate([keys, values], axis=1), 'ctx', axis=0, ti...  30.5 us
    all_gather x1, waiting for transfers between devices, local(): grad_out = lax.all_gather(grad_arrived, 'ctx', axis=0, tiled=True)  30 us
    all_to_all x1, blocking collectives, local(): lax.all_to_all(grad_slots.reshape(n_exp, capacity, width), 'exp', split_a...  18 us
    all_gather x1, waiting for transfers between devices, local(): expert_in = lax.all_gather(arrived, 'ctx', axis=0, tiled=True)  16.1 us
    all_to_all x1, blocking collectives, local(): lax.all_to_all(send.reshape(n_exp, capacity, width), 'exp', split_axis=0,...  13.6 us
    all_to_all x1, starting transfers between devices, local(): lax.all_to_all(grad_summed.reshape(n_exp, capacity, width), 'exp', split_...  7.52 us
  transfers between devices with their start and end apart: 8, of which 6 were waited for; matrix products, arithmetic and copies ran while one was open for 17% of the time, Pallas kernels for 0%

commit v1 on v0

--- a/solution.py
+++ b/solution.py
@@ -65,7 +65,9 @@
     arrived = lax.all_to_all(
         send.reshape(n_exp, capacity, width), "exp", split_axis=0, concat_axis=0, tiled=True
     ).reshape(slots, width)
-    expert_in = lax.all_gather(arrived, "ctx", axis=0, tiled=True)
+    expert_in = jnp.concatenate(
+        lax.all_to_all(jnp.stack([arrived] * lax.axis_size("ctx")), "ctx", 0, 0), axis=0
+    )
     gate_w = w_gate[0]
     up_w = w_up[0]
     down_w = w_down[0]

time: 340 us -> 329 us (0.968)
  waiting for transfers between devices: 186 us -> 110 us
  blocking collectives: 31.6 us -> 106 us
  starting transfers between devices: 22.8 us -> 15.1 us
    all_to_all x0 -> x2, blocking collectives: none -> 71.4 us  [the longest x1 59.2 us: local(): lax.all_to_all(jnp.stack([arrived] * lax.axis_size('ctx')), 'ctx', 0, 0)]
    all_gather x1, waiting for transfers between devices: 30 us -> 0.01 us  [local(): grad_out = lax.all_gather(grad_arrived, 'ctx', axis=0, tiled=True)]
    all_gather x1, waiting for transfers between devices: 30.5 us -> 9.34 us  [local(): lax.all_gather(jnp.concatenate([keys, values], axis=1), 'ctx', axis=0, ti...]
    all_gather x1 -> x0, waiting for transfers between devices: 16.1 us -> none  [local(): expert_in = lax.all_gather(arrived, 'ctx', axis=0, tiled=True)]
    all_to_all x1 -> x0, starting transfers between devices: 7.39 us -> none  [local(): lax.all_to_all(attended, 'exp', split_axis=0, concat_axis=1, tiled=True)]
    all_to_all x1 -> x0, waiting for transfers between devices: 5 us -> none  [local(): lax.all_to_all(attended, 'exp', split_axis=0, concat_axis=1, tiled=True)]
    all_to_all x1, blocking collectives: 13.6 us -> 18.5 us  [local(): lax.all_to_all(send.reshape(n_exp, capacity, width), 'exp', split_axis=0,...]
    reduce_scatter x1, waiting for transfers between devices: 51.4 us -> 47.6 us  [local(): lax.psum_scatter(jnp.dot(hidden, down_w, preferred_element_type=jnp.float...]
  transfers between devices with their start and end apart: 8 -> 6, of which waited for: 6 -> 3; matrix products, arithmetic and copies ran while one was open for 17% -> 19% of each run, Pallas kernels for 0% -> 0%
where the time goes in v1:
time: 329 us; the launch traced here: 328 us
  waiting for transfers between devices  110 us (33%)
  blocking collectives  106 us (32%)
  matrix products  56.8 us (17%)
  local copies, waits for them, and re-layouts  19.7 us (6%)
  starting transfers between devices  15.1 us (5%)
  between operations  13.9 us (4%)
  other arithmetic  6.21 us (2%)
    all_to_all x1, blocking collectives, local(): lax.all_to_all(jnp.stack([arrived] * lax.axis_size('ctx')), 'ctx', 0, 0)  59.2 us
    reduce_scatter x1, waiting for transfers between devices, local(): lax.psum_scatter((term + lax.dot_general(grad_up_pre, up_w, (((1,), (1,))...  52.9 us
    reduce_scatter x1, waiting for transfers between devices, local(): lax.psum_scatter(jnp.dot(hidden, down_w, preferred_element_type=jnp.float...  47.6 us
    all_to_all x1, blocking collectives, local(): lax.all_to_all(send.reshape(n_exp, capacity, width), 'exp', split_axis=0,...  18.5 us
    all_to_all x1, blocking collectives, local(): lax.all_to_all(grad_slots.reshape(n_exp, capacity, width), 'exp', split_a...  16.4 us
    all_to_all x1, blocking collectives, local(): lax.all_to_all(attended, 'exp', split_axis=0, concat_axis=1, tiled=True)  12.2 us
    all_gather x1, waiting for transfers between devices, local(): lax.all_gather(jnp.concatenate([keys, values], axis=1), 'ctx', axis=0, ti...  9.34 us
    all_to_all x1, starting transfers between devices, local(): lax.all_to_all(expert_out.reshape(n_exp, capacity, width), 'exp', split_a...  7.41 us
  transfers between devices with their start and end apart: 6, of which 3 were waited for; matrix products, arithmetic and copies ran while one was open for 19% of the time, Pallas kernels for 0%

profile of v1, /device:TPU:16, one launch (start us, length us, event | category | flops | bytes accessed | tf_op | source)
XLA Modules:
  0.0 328.1 jit_solution(2335261034715704574)
XLA Ops:
  7.2 1.6 pad_maximum_fusion
  8.9 0.8 copy.35
  9.8 0.2 select_reduce_fusion.1
  10.2 0.7 reduce_max.18
  10.9 0.7 fusion.33
  11.6 0.7 fusion.32
  12.3 0.7 multiply_add_fusion
  13.1 2.0 convolution_convert_fusion.4
  15.1 1.1 reshape.117
  16.2 16.4 %all_to_all.35 = bf16[8,6,3072]{2,1,0:T(8,128)(2,1)} all-to-all(bf16[8,6,3072]{2,1,0:T(8,128)(2,1)S(1)} %reshape.117), channel_id=1, replica_groups=mesh['ctx'=16,'exp'=8] {'exp'}, dimensions={0} | all-to-all | bytes 589824 | tf_op jit(solution)/shard_map/all_to_all | solution.py:95
  32.6 1.8 reshape.118
  34.5 1.0 copy.37
  35.5 0.1 copy.38
  35.7 9.3 %all-gather.3.cloned.1.call-done = bf16[2048,256]{1,0:T(8,128)(2,1)} async-done(((bf16[128,256]{1,0:T(8,128)(2,1)}), bf16[2048,256]{1,0:T(8,128)(2,1)}) %all-gather.3.cloned.1.call-update) | async-done | bytes 1048592 | tf_op jit(solution)/shard_map/all_gather | solution.py:23
  45.0 1.8 fusion.35
  46.8 0.5 fusion.13
  47.4 0.6 fusion.22
  48.2 12.2 %all_to_all.36 = bf16[8,16,384]{2,1,0:T(8,128)(2,1)S(1)} all-to-all(bf16[8,16,384]{2,1,0:T(8,128)(2,1)S(1)} %convert_element_type.88), channel_id=1, replica_groups=mesh['ctx'=16,'exp'=8] {'exp'}, dimensions={0} | all-to-all | bytes 196608 | tf_op jit(solution)/shard_map/all_to_all | solution.py:46
  60.4 0.1 fusion.27
  60.6 1.0 convolution_convert_fusion.5
  61.6 1.8 reshape.113
  63.4 18.5 %all_to_all.37 = bf16[8,6,3072]{2,1,0:T(8,128)(2,1)} all-to-all(bf16[8,6,3072]{2,1,0:T(8,128)(2,1)} %reshape.113), channel_id=1, replica_groups=mesh['ctx'=16,'exp'=8] {'exp'}, dimensions={0} | all-to-all | bytes 589824 | tf_op jit(solution)/shard_map/all_to_all | solution.py:65
  81.9 1.8 stack_reshape.2
  83.8 1.5 stack.3
  85.3 59.2 %all_to_all.38 = bf16[16,48,3072]{2,1,0:T(8,128)(2,1)S(1)} all-to-all(bf16[16,48,3072]{2,1,0:T(8,128)(2,1)S(1)} %stack.3), channel_id=1, replica_groups=mesh['ctx'=16,'exp'=8] {'ctx'}, dimensions={0} | all-to-all | bytes 9437184 | tf_op jit(solution)/shard_map/all_to_all | solution.py:69
  144.5 3.7 %fusion.7 = f32[768,512]{1,0:T(8,128)} fusion(bf16[768,3072]{1,0:T(8,128)(2,1)S(1)} %bitcast.59, bf16[1,3072,512]{2,1,0:T(8,128)(2,1)S(1)} %copy-done.3), kind=kOutput, calls=%fused_computation.16 | convolution fusion | flops 2415919104 | bytes 9437184 | tf_op jit(solution)/shard_map/dot_general | solution.py:75
  148.2 3.7 %fusion.11 = f32[768,512]{1,0:T(8,128)} fusion(bf16[768,3072]{1,0:T(8,128)(2,1)S(1)} %bitcast.60, bf16[1,3072,512]{2,1,0:T(8,128)(2,1)S(1)} %copy-done.9), kind=kOutput, calls=%fused_computation.20 | convolution fusion | flops 2415919104 | bytes 9437184 | tf_op jit(solution)/shard_map/dot_general | solution.py:74
  152.0 7.0 %multiply_convert_fusion = (bf16[768,512]{1,0:T(8,128)(2,1)}, bf16[768,512]{1,0:T(8,128)(2,1)}, bf16[768,512]{1,0:T(8,128)(2,1)S(1)}) fusion(f32[768,512]{1,0:T(8,128)} %fusion.11, f32[768,512]{1,0:T(8,128)} %fusion.7, bf16[768,3072]{1,0:T(8,128)(2,1)} %all-gather.5.cloned.1.call-done, bf16[1,512,3072]{2,1,0:T(8,128)(2,1)S(1)} %copy-done), kind=kOutput, calls=%fused_computation.28 | convolution fusion | flops 2421817344 | bytes 13369344 | tf_op jit(solution)/shard_map/dot_general | solution.py:100
  159.0 0.9 copy-done.11
  159.9 4.2 %convolution_convert_fusion = bf16[768,3072]{1,0:T(8,128)(2,1)} fusion(bf16[768,512]{1,0:T(8,128)(2,1)S(1)} %get-tuple-element.9, bf16[1,512,3072]{2,1,0:T(8,128)(2,1)S(1)} %copy-done), kind=kOutput, calls=%fused_computation.1 | convolution fusion | flops 2418278400 | bytes 8650752 | tf_op jit(solution)/shard_map/dot_general | solution.py:78
  164.1 0.2 reduce-scatter.5.cloned.1.call-start
  164.4 4.9 %fusion.9 = f32[768,3072]{1,0:T(8,128)S(1)} fusion(bf16[768,512]{1,0:T(8,128)(2,1)} %get-tuple-element.8, bf16[1,3072,512]{2,1,0:T(8,128)(2,1)} %param.17), kind=kOutput, calls=%fused_computation.18 | convolution fusion | flops 2415919104 | bytes 13369344 | tf_op jit(solution)/shard_map/dot_general | solution.py:117
  169.3 4.4 %add_convert_fusion = bf16[768,3072]{1,0:T(8,128)(2,1)} fusion(f32[768,3072]{1,0:T(8,128)S(1)} %fusion.9, bf16[768,512]{1,0:T(8,128)(2,1)S(1)} %copy-done.5, bf16[1,3072,512]{2,1,0:T(8,128)(2,1)S(1)} %copy-done.4), kind=kOutput, calls=%fused_computation | convolution fusion | flops 2420637696 | bytes 18087936 | tf_op jit(solution)/shard_map/dot_general | solution.py:123
  173.8 1.1 copy-done.6
  174.9 6.6 %fusion.1 = bf16[1,3072,512]{2,1,0:T(8,128)(2,1)} fusion(bf16[768,3072]{1,0:T(8,128)(2,1)} %bitcast.61, bf16[768,512]{1,0:T(8,128)(2,1)S(1)} %copy-done.6), kind=kOutput, calls=%fused_computation.6 | convolution fusion | flops 2417491968 | bytes 8650752 | tf_op jit(solution)/shard_map/dot_general | solution.py:114
  181.4 47.6 %reduce-scatter.3.cloned.1.call-done = bf16[48,3072]{1,0:T(8,128)(2,1)} async-done(((bf16[768,3072]{1,0:T(8,128)(2,1)}), bf16[48,3072]{1,0:T(8,128)(2,1)}) %reduce-scatter.3.cloned.1.call-update) | async-done | bytes 294928 | tf_op jit(solution)/shard_map/reduce_scatter | solution.py:77
  229.1 1.8 reshape.115
  230.9 7.4 %all-to-all-start.3 = ((bf16[8,6,3072]{2,1,0:T(8,128)(2,1)}), bf16[8,6,3072]{2,1,0:T(8,128)(2,1)}, u32[]{:S(2)}, u32[]{:S(2)}) async-start(bf16[8,6,3072]{2,1,0:T(8,128)(2,1)} %reshape.115), calls=%async_computation.4 | async-start | bytes 786432 | tf_op jit(solution)/shard_map/all_to_all | solution.py:83
  238.3 6.6 %fusion = bf16[1,3072,512]{2,1,0:T(8,128)(2,1)} fusion(bf16[768,3072]{1,0:T(8,128)(2,1)} %bitcast.62, bf16[768,512]{1,0:T(8,128)(2,1)S(1)} %copy-done.10), kind=kOutput, calls=%fused_computation.5 | convolution fusion | flops 2417491968 | bytes 8650752 | tf_op jit(solution)/shard_map/dot_general | solution.py:111
  244.9 52.9 %reduce-scatter.5.cloned.1.call-done = bf16[48,3072]{1,0:T(8,128)(2,1)} async-done(((bf16[768,3072]{1,0:T(8,128)(2,1)}), bf16[48,3072]{1,0:T(8,128)(2,1)}) %reduce-scatter.5.cloned.1.call-update) | async-done | bytes 294928 | tf_op jit(solution)/shard_map/reduce_scatter | solution.py:120
  297.7 1.8 reshape.119
  299.6 7.4 %all-to-all-start.5 = ((bf16[8,6,3072]{2,1,0:T(8,128)(2,1)}), bf16[8,6,3072]{2,1,0:T(8,128)(2,1)}, u32[]{:S(2)}, u32[]{:S(2)}) async-start(bf16[8,6,3072]{2,1,0:T(8,128)(2,1)} %reshape.119), calls=%async_computation.7 | async-start | bytes 786432 | tf_op jit(solution)/shard_map/all_to_all | solution.py:131
  306.9 7.0 %fusion.2 = bf16[1,512,3072]{2,1,0:T(8,128)(2,1)} fusion(bf16[768,512]{1,0:T(8,128)(2,1)} %copy-done.11, bf16[768,3072]{1,0:T(8,128)(2,1)} %all-gather.5.cloned.1.call-done), kind=kOutput, calls=%fused_computation.7 | convolution fusion | flops 2417491968 | bytes 8650752 | tf_op jit(solution)/shard_map/dot_general | solution.py:103
  314.0 1.8 reshape.116
  315.8 1.9 convolution_convert_fusion.6
  317.6 1.8 reshape.120
  319.4 1.3 multiply_reduce_fusion
  320.8 0.7 subtract_convert_fusion
  (45 shorter events, 0.9 us)
Async XLA Ops:
  7.2 144.8 %copy-start = (bf16[1,512,3072]{2,1,0:T(8,128)(2,1)S(1)}, bf16[1,512,3072]{2,1,0:T(8,128)(2,1)}, u32[]{:S(2)}) copy-start(bf16[1,512,3072]{2,1,0:T(8,128)(2,1)} %param.19) | copy-start | bytes 9437188
  7.2 37.8 %all-gather.3.cloned.1.call-start = ((), (), s32[]{:S(2)}) async-start(), calls=%async_computation.8 | async-start | bytes 1114112 | tf_op jit(solution)/shard_map/all_gather | solution.py:23
  8.8 143.1 %all-gather.5.cloned.1.call-start = ((), (), s32[]{:S(2)}) async-start(), calls=%async_computation.10 | async-start | bytes 5013504 | tf_op jit(solution)/shard_map/all_gather | solution.py:98
  34.5 194.6 %reduce-scatter.3.cloned.1.call-start = ((), (), s32[]{:S(2)}) async-start(), calls=%async_computation.9 | async-start | bytes 5013504 | tf_op jit(solution)/shard_map/reduce_scatter | solution.py:77
  45.0 2.3 copy-start.7
  47.4 13.2 %copy-start.8 = (f32[3072]{0:T(1024)S(1)}, f32[3072]{0:T(1024)}, u32[]{:S(2)}) copy-start(f32[3072]{0:T(1024)} %param.13) | copy-start | bytes 36868
  85.3 59.2 %copy-start.3 = (bf16[1,3072,512]{2,1,0:T(8,128)(2,1)S(1)}, bf16[1,3072,512]{2,1,0:T(8,128)(2,1)}, u32[]{:S(2)}) copy-start(bf16[1,3072,512]{2,1,0:T(8,128)(2,1)} %param.18) | copy-start | bytes 9437188
  144.5 3.7 %copy-start.2 = (bf16[16,48,3072]{2,1,0:T(8,128)(2,1)}, bf16[16,48,3072]{2,1,0:T(8,128)(2,1)S(1)}, u32[]{:S(2)}) copy-start(bf16[16,48,3072]{2,1,0:T(8,128)(2,1)S(1)} %all_to_all.38) | copy-start | bytes 14155780
  144.5 3.7 %copy-start.9 = (bf16[1,3072,512]{2,1,0:T(8,128)(2,1)S(1)}, bf16[1,3072,512]{2,1,0:T(8,128)(2,1)}, u32[]{:S(2)}) copy-start(bf16[1,3072,512]{2,1,0:T(8,128)(2,1)} %param.17) | copy-start | bytes 9437188
  159.0 0.9 copy-start.11
  164.1 133.6 %reduce-scatter.5.cloned.1.call-start = ((), (), s32[]{:S(2)}) async-start(), calls=%async_computation.11 | async-start | bytes 5013504 | tf_op jit(solution)/shard_map/reduce_scatter | solution.py:120
  164.4 4.9 %copy-start.4 = (bf16[1,3072,512]{2,1,0:T(8,128)(2,1)S(1)}, bf16[1,3072,512]{2,1,0:T(8,128)(2,1)}, u32[]{:S(2)}) copy-start(bf16[1,3072,512]{2,1,0:T(8,128)(2,1)} %param.18) | copy-start | bytes 9437188
  164.4 4.9 %copy-start.5 = (bf16[768,512]{1,0:T(8,128)(2,1)S(1)}, bf16[768,512]{1,0:T(8,128)(2,1)}, u32[]{:S(2)}) copy-start(bf16[768,512]{1,0:T(8,128)(2,1)} %get-tuple-element.7) | copy-start | bytes 2359300
  173.7 1.1 copy-start.6
  174.9 63.4 %copy-start.10 = (bf16[768,512]{1,0:T(8,128)(2,1)S(1)}, bf16[768,512]{1,0:T(8,128)(2,1)}, u32[]{:S(2)}) copy-start(bf16[768,512]{1,0:T(8,128)(2,1)} %get-tuple-element.8) | copy-start | bytes 2359300
  230.9 68.7 %all-to-all-start.3 = ((bf16[8,6,3072]{2,1,0:T(8,128)(2,1)}), bf16[8,6,3072]{2,1,0:T(8,128)(2,1)}, u32[]{:S(2)}, u32[]{:S(2)}) async-start(bf16[8,6,3072]{2,1,0:T(8,128)(2,1)} %reshape.115), calls=%async_computation.4 | async-start | bytes 786432 | tf_op jit(solution)/shard_map/all_to_all | solution.py:83
  299.6 18.1 %all-to-all-start.5 = ((bf16[8,6,3072]{2,1,0:T(8,128)(2,1)}), bf16[8,6,3072]{2,1,0:T(8,128)(2,1)}, u32[]{:S(2)}, u32[]{:S(2)}) async-start(bf16[8,6,3072]{2,1,0:T(8,128)(2,1)} %reshape.119), calls=%async_computation.7 | async-start | bytes 786432 | tf_op jit(solution)/shard_map/all_to_all | solution.py:131
  306.9 14.6 %copy-start.1 = (bf16[1,512,3072]{2,1,0:T(8,128)(2,1)S(1)}, bf16[1,512,3072]{2,1,0:T(8,128)(2,1)}, u32[]{:S(2)}) copy-start(bf16[1,512,3072]{2,1,0:T(8,128)(2,1)} %param.19) | copy-start | bytes 9437188
Sparse Core Ops, SparseCore 0:
  10.3 34.6 all-gather.2
  47.3 41.7 all-gather.4
  164.3 64.7 reduce-scatter.2
  231.3 66.3 reduce-scatter.4
